TPU v7x, 32 devices: a whole 2x2x4 slice. The times are simulated.
32 devices in a mesh: beam: 2 (over y), sub: 8 (over z, x), tm: 2 (over core).
Axes of the slice: x: 2, y: 2, z: 4, core: 2. Of those that a mesh axis runs over, the one named last changes fastest.
Arguments:
- filterbank: bfloat16 [2048, 1024], P(('beam', 'sub'), 'tm'), parts along dimension 0, may hold values from -6 to 6
- bandpass: float32 [2048], P(('beam', 'sub')), parts along dimension 0, may hold values from 0.3 to 3
- local_delays: int32 [7, 1024], P(None, 'sub'), may hold values from 0 to 32, as said below
- cross_delays: int32 [3, 128], P(None, 'sub'), may hold values from 0 to 32, as said below
Outputs:
- dedispersed: float32 [256, 1024], P(('beam', 'sub'), 'tm'), parts along dimension 0
There are 2 independent parts, one for each index of `beam`. A program takes and returns all parts, laid end to end along the dimension named above; an argument that names none is the same for every part. Nothing has to cross between parts.
Inputs may be any that keep to these rules, and one draw needn't show every extreme that they name: `local_delays`: whole samples; level m of the local levels reads its first entries of each block of 128. `cross_delays`: whole samples.
All inputs are finite; a program needn't handle non-finite values.
Results may differ from a plain program's by a relative error of at most 0.0003.
Values may be sent and summed in bfloat16 or wider, within the bound.
A program may use at most 64 MiB of HBM per device.

v0:
```python
import math

import jax
import jax.numpy as jnp
from jax import lax
from jax.sharding import PartitionSpec as P


def passed_along(block, axis, distance):
    devices = range(lax.axis_size(axis))
    route = [(i - distance, i) for i in devices if i - distance in devices]
    return lax.ppermute(block, axis, route)


def swapped(x, axis, apart):
    return lax.ppermute(x, axis, [(i, i ^ 1 << apart) for i in range(lax.axis_size(axis))])


def earlier_cols(upper, shift_max):
    return jnp.zeros((upper.shape[0], shift_max), upper.dtype)


def delayed(upper, rim_cols, delays):
    row_count = upper.shape[0]
    shift_max = rim_cols.shape[1]
    shifted = jnp.concatenate([rim_cols, upper], axis=1)
    total_cols = shifted.shape[1]
    for bit_index in range(shift_max.bit_length()):
        step_size = 1 << bit_index
        if step_size >= total_cols:
            continue
        moving = jnp.concatenate(
            [
                jnp.zeros((row_count, step_size), shifted.dtype),
                shifted[:, : total_cols - step_size],
            ],
            axis=1,
        )
        selector = delays >> bit_index & 1 == 1
        shifted = jnp.where(selector[:, None], moving, shifted)
    return shifted[:, shift_max:]


def shards(filterbank, bandpass, local_delays, cross_delays):
    span_time = filterbank.shape[1]
    shift_max = span_time // 16
    local_levels = local_delays.shape[0]
    cross_levels = lax.axis_size("sub").bit_length() - 1
    trials_dev = cross_delays.shape[1]
    reach = 0
    reach = (local_levels + cross_levels) * shift_max
    before = passed_along(filterbank[:, span_time - reach - 15 :], "tm", 1)
    after = passed_along(filterbank[:, :15], "tm", -1)
    padded = jnp.concatenate([before, filterbank, after], axis=1)
    corrected = padded.astype(jnp.float32) * bandpass[:, None]
    window_total = lax.reduce_window(
        corrected, jnp.zeros((), corrected.dtype), lax.add, (1, 31), (1, 1), "VALID"
    )
    current = corrected[:, 15 : corrected.shape[1] - 15] - window_total / 31.0
    column_pos = lax.broadcasted_iota(jnp.int32, current.shape, 1)
    outside = jnp.logical_and(column_pos < reach, lax.axis_index("tm") == 0)
    current = jnp.where(outside, jnp.zeros((), current.dtype), current)
    span_cols = current.shape[1]
    trial_count = 1
    for level_index in range(local_levels):
        band_count = current.shape[0] // trial_count
        grouped = current.reshape(band_count // 2, 2, trial_count, span_cols)
        lower = grouped[:, 0]
        upper = grouped[:, 1]
        rim_cols = earlier_cols(upper.reshape(-1, span_cols), shift_max).reshape(
            band_count // 2, trial_count, shift_max
        )
        new_count = min(2 * trial_count, trials_dev)
        if new_count > trial_count:
            lower = jnp.concatenate([lower, lower], axis=1)
            upper = jnp.concatenate([upper, upper], axis=1)
            rim_cols = jnp.concatenate([rim_cols, rim_cols], axis=1)
        row_total = band_count // 2 * new_count
        delays = local_delays[level_index, :row_total]
        current = lower.reshape(row_total, span_cols) + delayed(
            upper.reshape(row_total, span_cols), rim_cols.reshape(row_total, shift_max), delays
        )
        trial_count = new_count
    position = lax.axis_index("sub")
    for level_index in range(cross_levels):
        partner = swapped(current, "sub", level_index)
        upper_side = position >> level_index & 1 == 1
        lower = jnp.where(upper_side, partner, current)
        upper = jnp.where(upper_side, current, partner)
        rim_cols = earlier_cols(upper, shift_max)
        current = lower + delayed(upper, rim_cols, cross_delays[level_index])
    norm_scale = 1.0 / math.sqrt(filterbank.shape[0] * lax.axis_size("sub"))
    return current[:, span_cols - span_time :] * norm_scale


def solution(mesh):
    return jax.shard_map(
        shards,
        mesh=mesh,
        in_specs=(P(("beam", "sub"), "tm"), P(("beam", "sub")), P(None, "sub"), P(None, "sub")),
        out_specs=P(("beam", "sub"), "tm"),
        check_vma=False,
    )
```

profile of v0, /device:TPU:0, one launch (start us, length us, event | category | flops | bytes accessed | tf_op | source)
XLA Modules:
  0.0 39.8 jit_solution(2519864000627640307)
XLA Ops:
  0.0 1.0 %copy.14 = bf16[128,512]{0,1:T(8,128)(2,1)S(1)} copy(bf16[128,512]{1,0:T(8,128)(2,1)} %param.4) | data formatting | bytes 262144 | tf_op args[0]
  1.1 2.4 %collective-permute-start = (bf16[128,335]{0,1:T(8,128)(2,1)S(1)}, bf16[128,335]{0,1:T(8,128)(2,1)S(1)}, u32[]{:S(2)}, u32[]{:S(2)}) collective-permute-start(bf16[128,335]{0,1:T(8,128)(2,1)S(1)} %slice.392), channel_id=1, source_target_pairs={{0,1},{2,3},{4,5},{6,7},{8,9},{10,11},{12,13},{14,15},{16,17},{18,... | collective-permute-start | bytes 257288 | tf_op jit(solution)/shard_map/ppermute | solution.py:12
  3.5 1.3 %collective-permute-start.1 = (bf16[128,15]{0,1:T(8,128)(2,1)S(1)}, bf16[128,15]{0,1:T(8,128)(2,1)S(1)}, u32[]{:S(2)}, u32[]{:S(2)}) collective-permute-start(bf16[128,15]{0,1:T(8,128)(2,1)S(1)} %slice.393), channel_id=1, source_target_pairs={{1,0},{3,2},{5,4},{7,6},{9,8},{11,10},{13,12},{15,14},{17,16},{19,... | collective-permute-start | bytes 11528 | tf_op jit(solution)/shard_map/ppermute | solution.py:12
  4.9 1.6 %collective-permute-done.1 = bf16[128,15]{0,1:T(8,128)(2,1)S(1)} collective-permute-done((bf16[128,15]{0,1:T(8,128)(2,1)S(1)}, bf16[128,15]{0,1:T(8,128)(2,1)S(1)}, u32[]{:S(2)}, u32[]{:S(2)}) %collective-permute-start.1) | collective-permute-done | bytes 3872 | tf_op jit(solution)/shard_map/ppermute | solution.py:12
  6.6 3.5 %reduce_window.7 = f32[128,832]{0,1:T(8,128)S(1)} reduce-window(f32[128,862]{0,1:T(8,128)S(1)} %convert_multiply_fusion, f32[]{:T(128)} %constant.18.clone.1), window={size=1x31}, to_apply=%region_0.0 | reduce-window | flops 3194880 | bytes 867332 | tf_op jit(solution)/shard_map/reduce_window | solution.py:56
  10.3 0.2 copy.17
  10.5 0.3 reshape.826
  10.8 0.4 fusion.14
  11.2 0.4 copy.19
  11.6 0.3 reshape.828
  11.9 0.2 pad_slice_fusion.3
  12.1 0.4 copy.18
  12.5 0.3 reshape.827
  12.8 0.3 pad_select_fusion.19
  13.2 0.2 pad_select_fusion.18
  13.4 0.2 pad_select_fusion.17
  13.6 0.2 pad_select_fusion.16
  13.8 0.2 pad_select_fusion.15
  14.0 0.2 fusion.3
  14.2 0.3 reshape.829
  14.9 0.2 pad_slice_fusion.2
  15.4 0.3 pad_select_fusion.14
  15.8 0.2 pad_select_fusion.13
  16.0 0.2 pad_select_fusion.12
  16.2 0.2 pad_select_fusion.11
  16.4 0.2 pad_select_fusion.10
  16.6 0.2 fusion.2
  17.1 0.2 pad_slice_fusion.1
  17.3 0.3 pad_select_fusion.9
  17.6 0.2 pad_select_fusion.8
  17.8 0.2 pad_select_fusion.7
  18.0 0.2 pad_select_fusion.6
  18.2 0.2 pad_select_fusion.5
  18.4 0.2 fusion.1
  18.9 0.5 %pad_select_fusion.4 = f32[128,864]{1,0:T(8,128)S(1)} fusion(f32[128,863]{1,0:T(8,128)S(1)} %pad_slice_fusion, f32[128,832]{1,0:T(8,128)S(1)} %bitcast.215, pred[128]{0:T(512)(128)(4,1)S(1)} %get-tuple-element.57), kind=kLoop, calls=%fused_computation.20 | loop fusion | flops 110592 | bytes 1310336 | tf_op jit(solution)/shard_map/jit(_where)/select_n | solution.py:40
  19.4 0.2 pad_select_fusion.3
  19.6 0.2 pad_select_fusion.2
  19.8 0.2 pad_select_fusion.1
  20.1 0.2 pad_select_fusion
  20.3 0.2 fusion
  20.6 0.2 pad_select_fusion.24
  23.0 2.4 %collective-permute-start.2 = (f32[16,832]{1,0:T(8,128)S(1)}, f32[16,832]{1,0:T(8,128)S(1)}, u32[]{:S(2)}, u32[]{:S(2)}) collective-permute-start(f32[16,832]{1,0:T(8,128)S(1)} %fusion.9), channel_id=1, source_target_pairs={{0,2},{2,0},{4,6},{6,4},{8,10},{10,8},{12,14},{14,12},{1,3},{3,1},... | collective-permute-start | bytes 159752 | tf_op jit(solution)/shard_map/ppermute | solution.py:16
  25.4 2.2 %collective-permute-done.2 = f32[16,832]{1,0:T(8,128)S(1)} collective-permute-done((f32[16,832]{1,0:T(8,128)S(1)}, f32[16,832]{1,0:T(8,128)S(1)}, u32[]{:S(2)}, u32[]{:S(2)}) %collective-permute-start.2) | collective-permute-done | bytes 53280 | tf_op jit(solution)/shard_map/ppermute | solution.py:16
  28.3 2.1 %collective-permute-start.3 = (f32[16,832]{1,0:T(8,128)S(1)}, f32[16,832]{1,0:T(8,128)S(1)}, u32[]{:S(2)}, u32[]{:S(2)}) collective-permute-start(f32[16,832]{1,0:T(8,128)S(1)} %fusion.8), channel_id=1, source_target_pairs={{0,4},{2,6},{4,0},{6,2},{8,12},{10,14},{12,8},{14,10},{1,5},{3,7},... | collective-permute-start | bytes 159752 | tf_op jit(solution)/shard_map/ppermute | solution.py:16
  30.3 2.2 %collective-permute-done.3 = f32[16,832]{1,0:T(8,128)S(1)} collective-permute-done((f32[16,832]{1,0:T(8,128)S(1)}, f32[16,832]{1,0:T(8,128)S(1)}, u32[]{:S(2)}, u32[]{:S(2)}) %collective-permute-start.3) | collective-permute-done | bytes 53280 | tf_op jit(solution)/shard_map/ppermute | solution.py:16
  33.2 3.1 %collective-permute-start.4 = (f32[16,832]{1,0:T(8,128)S(1)}, f32[16,832]{1,0:T(8,128)S(1)}, u32[]{:S(2)}, u32[]{:S(2)}) collective-permute-start(f32[16,832]{1,0:T(8,128)S(1)} %fusion.7), channel_id=1, source_target_pairs={{0,8},{2,10},{4,12},{6,14},{8,0},{10,2},{12,4},{14,6},{1,9},{3,11}... | collective-permute-start | bytes 159752 | tf_op jit(solution)/shard_map/ppermute | solution.py:16
  36.3 2.2 %collective-permute-done.4 = f32[16,832]{1,0:T(8,128)S(1)} collective-permute-done((f32[16,832]{1,0:T(8,128)S(1)}, f32[16,832]{1,0:T(8,128)S(1)}, u32[]{:S(2)}, u32[]{:S(2)}) %collective-permute-start.4) | collective-permute-done | bytes 53280 | tf_op jit(solution)/shard_map/ppermute | solution.py:16
  39.1 0.7 %fusion.11 = f32[16,512]{1,0:T(8,128)} fusion(f32[16,832]{1,0:T(8,128)S(1)} %get-tuple-element.18, f32[16,832]{1,0:T(8,128)S(1)} %get-tuple-element.17, f32[16,832]{1,0:T(8,128)S(1)} %fusion.7, f32[16,832]{1,0:T(8,128)S(1)} %collective-permute-done.4, pred[16]{0:T(512)(128)(4,1)S(1)} %get-tuple-element.61, pred[]{:T(512)S(6)} %eq.612), kind=kLoop, calls=%fused_computation.101 | loop fusion | flops 32768 | bytes 184337 | tf_op jit(solution)/shard_map/mul | solution.py:93
  (80 shorter events, 5.7 us)
Async XLA Ops:
  1.1 3.7 %copy-start = (s32[7,128]{1,0:T(8,128)S(1)}, s32[7,128]{1,0:T(8,128)}, u32[]{:S(2)}) copy-start(s32[7,128]{1,0:T(8,128)} %param.6) | copy-start | bytes 10756
  1.1 5.5 %collective-permute-start = (bf16[128,335]{0,1:T(8,128)(2,1)S(1)}, bf16[128,335]{0,1:T(8,128)(2,1)S(1)}, u32[]{:S(2)}, u32[]{:S(2)}) collective-permute-start(bf16[128,335]{0,1:T(8,128)(2,1)S(1)} %slice.392), channel_id=1, source_target_pairs={{0,1},{2,3},{4,5},{6,7},{8,9},{10,11},{12,13},{14,15},{16,17},{18,... | collective-permute-start | bytes 257288 | tf_op jit(solution)/shard_map/ppermute | solution.py:12
  3.5 3.1 %collective-permute-start.1 = (bf16[128,15]{0,1:T(8,128)(2,1)S(1)}, bf16[128,15]{0,1:T(8,128)(2,1)S(1)}, u32[]{:S(2)}, u32[]{:S(2)}) collective-permute-start(bf16[128,15]{0,1:T(8,128)(2,1)S(1)} %slice.393), channel_id=1, source_target_pairs={{1,0},{3,2},{5,4},{7,6},{9,8},{11,10},{13,12},{15,14},{17,16},{19,... | collective-permute-start | bytes 11528 | tf_op jit(solution)/shard_map/ppermute | solution.py:12
  4.9 1.6 %copy-start.2 = (f32[128]{0:T(128)S(1)}, f32[128]{0:T(128)}, u32[]{:S(2)}) copy-start(f32[128]{0:T(128)} %param.5) | copy-start | bytes 1540
  22.9 2.5 %copy-start.1 = (s32[3,16]{1,0:T(4,128)S(1)}, s32[3,16]{1,0:T(4,128)}, u32[]{:S(2)}) copy-start(s32[3,16]{1,0:T(4,128)} %param.7) | copy-start | bytes 580
  23.0 4.6 %collective-permute-start.2 = (f32[16,832]{1,0:T(8,128)S(1)}, f32[16,832]{1,0:T(8,128)S(1)}, u32[]{:S(2)}, u32[]{:S(2)}) collective-permute-start(f32[16,832]{1,0:T(8,128)S(1)} %fusion.9), channel_id=1, source_target_pairs={{0,2},{2,0},{4,6},{6,4},{8,10},{10,8},{12,14},{14,12},{1,3},{3,1},... | collective-permute-start | bytes 159752 | tf_op jit(solution)/shard_map/ppermute | solution.py:16
  28.3 4.2 %collective-permute-start.3 = (f32[16,832]{1,0:T(8,128)S(1)}, f32[16,832]{1,0:T(8,128)S(1)}, u32[]{:S(2)}, u32[]{:S(2)}) collective-permute-start(f32[16,832]{1,0:T(8,128)S(1)} %fusion.8), channel_id=1, source_target_pairs={{0,4},{2,6},{4,0},{6,2},{8,12},{10,14},{12,8},{14,10},{1,5},{3,7},... | collective-permute-start | bytes 159752 | tf_op jit(solution)/shard_map/ppermute | solution.py:16
  33.2 5.3 %collective-permute-start.4 = (f32[16,832]{1,0:T(8,128)S(1)}, f32[16,832]{1,0:T(8,128)S(1)}, u32[]{:S(2)}, u32[]{:S(2)}) collective-permute-start(f32[16,832]{1,0:T(8,128)S(1)} %fusion.7), channel_id=1, source_target_pairs={{0,8},{2,10},{4,12},{6,14},{8,0},{10,2},{12,4},{14,6},{1,9},{3,11}... | collective-permute-start | bytes 159752 | tf_op jit(solution)/shard_map/ppermute | solution.py:16
where the time goes:
time: 40 us; the launch traced here: 39.8 us
  other arithmetic  14.2 us (36%)
  starting transfers between devices  11.2 us (28%)
  waiting for transfers between devices  8.15 us (20%)
  local copies, waits for them, and re-layouts  5.49 us (14%)
  between operations  0.75 us (2%)
    select_n x50, other arithmetic, delayed(): shifted = jnp.where(selector[:, None], moving, shifted)  7.69 us
    ppermute x3, starting transfers between devices, swapped(): lax.ppermute(x, axis, [(i, i ^ 1 << apart) for i in range(lax.axis_size(a...  7.55 us
    ppermute x3, waiting for transfers between devices, swapped(): lax.ppermute(x, axis, [(i, i ^ 1 << apart) for i in range(lax.axis_size(a...  6.54 us
    ppermute x2, starting transfers between devices, passed_along(): return lax.ppermute(block, axis, route)  3.69 us
    another operation x1, other arithmetic, shards(): lax.reduce_window(corrected, jnp.zeros((), corrected.dtype), lax.add, (1,...  3.52 us
    ppermute x2, waiting for transfers between devices, passed_along(): return lax.ppermute(block, axis, route)  1.61 us
    slice x11, local copies, waits for them, and re-layouts, delayed(): shifted[:, :total_cols - step_size]  1.32 us
    add x7, other arithmetic, shards(): lower.reshape(row_total, span_cols)  1.13 us
  transfers between devices with their start and end apart: 5, of which 4 were waited for; matrix products, arithmetic and copies ran while one was open for 0% of the time, Pallas kernels for 0%

commit v1 on v0

v1 whole, which is shorter than its diff:
```python
import functools
import math

import jax
import jax.numpy as jnp
from jax import lax
from jax.experimental import pallas as pl
from jax.experimental.pallas import tpu as pltpu
from jax.sharding import PartitionSpec as P

MESH = pl.DeviceIdType.MESH
LANES = 128
SUB = 8
HALF = 15
WINDOW = 31.0


def tiles_of(columns):
    return -(-columns // LANES)


def delayed(tiles, delay, lane, count):
    tiles = tiles[max(0, len(tiles) - count - 1) :]
    source = (lane - delay) & (LANES - 1)
    keep = lane >= delay
    turned = [jnp.take_along_axis(t, source, axis=1, mode="promise_in_bounds") for t in tiles]
    if len(turned) == count:
        turned = [jnp.zeros_like(turned[0])] + turned
    return [jnp.where(keep, turned[k + 1], turned[k]) for k in range(count)]


def kernel(
    geometry,
    fb_hbm, bp_hbm, ld_hbm, cd_hbm,
    out_ref,
    fpad, bp_v, ld_v, cd_v, x0, delay_l, delay_c, plane, sent, got,
    load_sem, halo_send, halo_recv, cross_send, cross_recv,
):
    channels, span, local_levels, cross_levels, trials, shift_max, norm = geometry
    own = span // LANES
    reach = (local_levels + cross_levels) * shift_max
    halo = tiles_of(reach + HALF)
    growth = trials.bit_length() - 1
    row_tiles = trials // SUB
    tm = lax.axis_index("tm")
    sub = lax.axis_index("sub")
    other = 1 - tm

    barrier = pltpu.get_barrier_semaphore()
    pl.semaphore_signal(barrier, inc=1, device_id={"tm": other}, device_id_type=MESH)
    for level in range(cross_levels):
        pl.semaphore_signal(barrier, inc=1, device_id={"sub": sub ^ (1 << level)}, device_id_type=MESH)

    first, last = halo * LANES, (halo + own) * LANES
    loads = [
        pltpu.make_async_copy(ld_hbm, ld_v, load_sem.at[0]),
        pltpu.make_async_copy(cd_hbm, cd_v, load_sem.at[1]),
        pltpu.make_async_copy(bp_hbm, bp_v, load_sem.at[2]),
        pltpu.make_async_copy(fb_hbm, fpad.at[:, first:last], load_sem.at[3]),
    ]
    for load in loads:
        load.start()

    @pl.when(tm == 0)
    def _():
        fpad[:, :first] = jnp.zeros((channels, first), fpad.dtype)

    @pl.when(tm == 1)
    def _():
        fpad[:, last:] = jnp.zeros((channels, LANES), fpad.dtype)

    pl.semaphore_wait(barrier, 1 + cross_levels)
    ahead = pltpu.make_async_remote_copy(
        src_ref=fb_hbm.at[:, span - first :], dst_ref=fpad.at[:, :first],
        send_sem=halo_send.at[0], recv_sem=halo_recv.at[0],
        device_id={"tm": other}, device_id_type=MESH,
    )
    back = pltpu.make_async_remote_copy(
        src_ref=fb_hbm.at[:, :LANES], dst_ref=fpad.at[:, last:],
        send_sem=halo_send.at[1], recv_sem=halo_recv.at[1],
        device_id={"tm": other}, device_id_type=MESH,
    )

    @pl.when(tm == 0)
    def _():
        ahead.start()

    @pl.when(tm == 1)
    def _():
        back.start()

    for load in loads[:3]:
        load.wait()
    ones = jnp.ones((channels, LANES), jnp.float32).astype(jnp.bfloat16)
    row_at = lax.broadcasted_iota(jnp.int32, (channels, channels), 0)
    col_at = lax.broadcasted_iota(jnp.int32, (channels, channels), 1)
    diagonal = row_at == col_at
    rows = channels
    for level in range(local_levels):
        if level >= growth:
            rows //= 2
        spread = jnp.where(diagonal[:rows], ld_v[level : level + 1, :].astype(jnp.float32), 0.0)
        spread = jnp.dot(spread.astype(jnp.bfloat16), ones, preferred_element_type=jnp.float32)
        delay_l[level, :rows, :] = spread.astype(jnp.int32)
    for level in range(cross_levels):
        spread = jnp.where(diagonal[:trials, :trials], cd_v[level : level + 1, :].astype(jnp.float32), 0.0)
        spread = jnp.dot(spread.astype(jnp.bfloat16), ones[:trials], preferred_element_type=jnp.float32)
        delay_c[level] = spread.astype(jnp.int32)
    gain = jnp.dot(
        jnp.where(diagonal, bp_v[...], 0.0), jnp.ones((channels, LANES), jnp.float32),
        precision=lax.Precision.HIGHEST, preferred_element_type=jnp.float32,
    )
    halo_gain = gain * tm.astype(jnp.float32)
    band_row = lax.broadcasted_iota(jnp.int32, (3 * LANES, LANES), 0)
    band_col = lax.broadcasted_iota(jnp.int32, (3 * LANES, LANES), 1)
    apart = band_row - LANES - band_col
    band = jnp.where((apart >= -HALF) & (apart <= HALF), 1.0, 0.0).astype(jnp.bfloat16)

    loads[3].wait()

    @pl.when(tm == 0)
    def _():
        ahead.wait_send()
        back.wait_recv()

    @pl.when(tm == 1)
    def _():
        back.wait_send()
        ahead.wait_recv()

    for k in range(halo + own):
        low = max(k - 1, 0)
        total = jnp.dot(
            fpad[:, low * LANES : (k + 2) * LANES], band[(low - k + 1) * LANES :],
            preferred_element_type=jnp.float32,
        )
        centre = fpad[:, k * LANES : (k + 1) * LANES].astype(jnp.float32)
        x0[:, k * LANES : (k + 1) * LANES] = (halo_gain if k < halo else gain) * (centre - total / WINDOW)

    lane = lax.broadcasted_iota(jnp.int32, (SUB, LANES), 1)
    sublane = lax.broadcasted_iota(jnp.int32, (SUB, LANES), 0)
    counts = [own + tiles_of(reach - (m + 1) * shift_max) for m in range(local_levels + cross_levels)]

    def block(at, carry):
        base = at * trials
        current = []
        for r in range(row_tiles):
            here = pl.ds(pl.multiple_of(base + r * SUB, SUB), SUB)
            current.append([x0[here, k * LANES : (k + 1) * LANES] for k in range(halo + own)])
        for level in range(growth):
            count, step = counts[level], 1 << level
            following = []
            for r in range(row_tiles):
                delay = delay_l[level, pl.ds(pl.multiple_of(base + r * SUB, SUB), SUB), :]
                if step < SUB:
                    is_upper = (sublane & step) != 0
                    lower, upper = [], []
                    for t in current[r]:
                        down = pltpu.roll(t, step, 0)
                        up = down if 2 * step == SUB else pltpu.roll(t, SUB - step, 0)
                        lower.append(jnp.where(is_upper, down, t))
                        upper.append(jnp.where(is_upper, t, up))
                else:
                    apart = step // SUB
                    lower, upper = current[r & ~apart], current[r | apart]
                moved = delayed(upper, delay, lane, count)
                following.append([a + b for a, b in zip(lower[len(lower) - count :], moved)])
            current = following
        for r in range(row_tiles):
            here = pl.ds(pl.multiple_of(base + r * SUB, SUB), SUB)
            for k, t in enumerate(current[r]):
                plane[here, k * LANES : (k + 1) * LANES] = t
        return carry

    lax.fori_loop(0, channels // trials, block, 0)

    bands = channels // trials
    count = counts[growth - 1]
    current = [
        [[plane[(b * row_tiles + r) * SUB : (b * row_tiles + r + 1) * SUB, k * LANES : (k + 1) * LANES] for k in range(count)] for r in range(row_tiles)]
        for b in range(bands)
    ]
    for level in range(growth, local_levels):
        count = counts[level]
        bands //= 2
        following = []
        for b in range(bands):
            made = []
            for r in range(row_tiles):
                at = (b * row_tiles + r) * SUB
                moved = delayed(current[2 * b + 1][r], delay_l[level, at : at + SUB, :], lane, count)
                lower = current[2 * b][r]
                made.append([x + y for x, y in zip(lower[len(lower) - count :], moved)])
            following.append(made)
        current = following
    rows_of = current[0]

    def exchange(level, r, skip):
        here = (level, pl.ds(r * SUB, SUB), pl.ds(skip * LANES, (width - skip) * LANES))
        return pltpu.make_async_remote_copy(
            src_ref=sent.at[here], dst_ref=got.at[here],
            send_sem=cross_send.at[level, r], recv_sem=cross_recv.at[level, r],
            device_id={"sub": sub ^ (1 << level)}, device_id_type=MESH,
        )

    width = len(rows_of[0])
    copies = []

    def send(level, r):
        skip = width - len(rows_of[r])
        for k, t in enumerate(rows_of[r], skip):
            sent[level, r * SUB : (r + 1) * SUB, k * LANES : (k + 1) * LANES] = t
        copy = exchange(level, r, skip)
        copy.start()
        copies.append(copy)
        return copy

    flight = [send(0, r) for r in range(row_tiles)] if cross_levels else []
    for level in range(cross_levels):
        count = counts[local_levels + level]
        on_top = (sub >> level) & 1 == 1
        for r in range(row_tiles):
            mine = rows_of[r]
            flight[r].wait_recv()
            skip = width - len(mine)
            theirs = [got[level, r * SUB : (r + 1) * SUB, (k + skip) * LANES : (k + skip + 1) * LANES] for k in range(len(mine))]
            lower = [jnp.where(on_top, t, m) for t, m in zip(theirs, mine)]
            upper = [jnp.where(on_top, m, t) for t, m in zip(theirs, mine)]
            moved = delayed(upper, delay_c[level, r * SUB : (r + 1) * SUB, :], lane, count)
            rows_of[r] = [x + y for x, y in zip(lower[len(lower) - count :], moved)]
            if level + 1 < cross_levels:
                flight[r] = send(level + 1, r)
    for r in range(row_tiles):
        for k, t in enumerate(rows_of[r][-own:]):
            out_ref[r * SUB : (r + 1) * SUB, k * LANES : (k + 1) * LANES] = t * norm
    for copy in copies:
        copy.wait_send()


def shards(filterbank, bandpass, local_delays, cross_delays):
    channels, span = filterbank.shape
    shift_max = span // 16
    local_levels = local_delays.shape[0]
    cross_levels = lax.axis_size("sub").bit_length() - 1
    trials = cross_delays.shape[1]
    norm = 1.0 / math.sqrt(channels * lax.axis_size("sub"))
    own = span // LANES
    reach = (local_levels + cross_levels) * shift_max
    halo = tiles_of(reach + HALF)
    width = (own + tiles_of(cross_levels * shift_max)) * LANES
    geometry = (channels, span, local_levels, cross_levels, trials, shift_max, norm)
    return pl.pallas_call(
        functools.partial(kernel, geometry),
        out_shape=jax.ShapeDtypeStruct((trials, span), jnp.float32),
        in_specs=[pl.BlockSpec(memory_space=pl.ANY)] * 4,
        out_specs=pl.BlockSpec(memory_space=pltpu.VMEM),
        scratch_shapes=[
            pltpu.VMEM((channels, (halo + own + 1) * LANES), jnp.bfloat16),
            pltpu.VMEM((1, channels), jnp.float32),
            pltpu.VMEM(local_delays.shape, jnp.int32),
            pltpu.VMEM(cross_delays.shape, jnp.int32),
            pltpu.VMEM((channels, (halo + own) * LANES), jnp.float32),
            pltpu.VMEM((local_levels, channels, LANES), jnp.int32),
            pltpu.VMEM((max(cross_levels, 1), trials, LANES), jnp.int32),
            pltpu.VMEM((channels, (halo + own) * LANES), jnp.float32),
            pltpu.VMEM((max(cross_levels, 1), trials, width), jnp.float32),
            pltpu.VMEM((max(cross_levels, 1), trials, width), jnp.float32),
            pltpu.SemaphoreType.DMA((4,)),
            pltpu.SemaphoreType.DMA((2,)),
            pltpu.SemaphoreType.DMA((2,)),
            pltpu.SemaphoreType.DMA((max(cross_levels, 1), trials // SUB)),
            pltpu.SemaphoreType.DMA((max(cross_levels, 1), trials // SUB)),
        ],
        compiler_params=pltpu.CompilerParams(collective_id=0, has_side_effects=True),
    )(filterbank, bandpass.reshape(1, channels), local_delays, cross_delays)


def solution(mesh):
    return jax.shard_map(
        shards,
        mesh=mesh,
        in_specs=(P(("beam", "sub"), "tm"), P(("beam", "sub")), P(None, "sub"), P(None, "sub")),
        out_specs=P(("beam", "sub"), "tm"),
        check_vma=False,
    )
```

time: 40 us -> 20.1 us (0.50)
  Pallas kernels: 0 us -> 18.5 us
  other arithmetic: 14.2 us -> 0 us
  starting transfers between devices: 11.2 us -> 0 us
  waiting for transfers between devices: 8.15 us -> 0 us
  local copies, waits for them, and re-layouts: 5.49 us -> 1.38 us
  between operations: 0.75 us -> 0.01 us
    pallas_call x0 -> x1, Pallas kernels: none -> 18.5 us  [shards(): pl.pallas_call(functools.partial(kernel, geometry), out_shape=jax.ShapeDt...]
    ppermute x5 -> x0, starting transfers between devices: 11.2 us -> none  [the longest x3 7.55 us: swapped(): lax.ppermute(x, axis, [(i, i ^ 1 << apart) for i in range(lax.axis_size(a...]
    ppermute x5 -> x0, waiting for transfers between devices: 8.15 us -> none  [the longest x3 6.54 us: swapped(): lax.ppermute(x, axis, [(i, i ^ 1 << apart) for i in range(lax.axis_size(a...]
    select_n x54 -> x0, other arithmetic: 7.89 us -> none  [the longest x50 7.69 us: delayed(): shifted = jnp.where(selector[:, None], moving, shifted)]
    another operation x1 -> x0, other arithmetic: 3.52 us -> none  [shards(): lax.reduce_window(corrected, jnp.zeros((), corrected.dtype), lax.add, (1,...]
    slice x16 -> x0, local copies, waits for them, and re-layouts: 1.76 us -> none  [the longest x11 1.32 us: delayed(): shifted[:, :total_cols - step_size]]
    reshape x7 -> x0, local copies, waits for them, and re-layouts: 1.61 us -> none  [the longest x3 0.66 us: shards(): grouped = current.reshape(band_count // 2, 2, trial_count, span_cols)]
    add x9 -> x0, other arithmetic: 1.32 us -> none  [the longest x7 1.13 us: shards(): lower.reshape(row_total, span_cols)]
  transfers between devices with their start and end apart: 5 -> 0, of which waited for: 4 -> 0; matrix products, arithmetic and copies ran while one was open for 0% -> 0% of each run, Pallas kernels for 0% -> 0%
where the time goes in v1:
time: 20.1 us; the launch traced here: 19.9 us
  Pallas kernels  18.5 us (92%)
  local copies, waits for them, and re-layouts  1.38 us (7%)
    pallas_call x1, Pallas kernels, shards(): pl.pallas_call(functools.partial(kernel, geometry), out_shape=jax.ShapeDt...  18.5 us
    unnamed x1, local copies, waits for them, and re-layouts  1.38 us

profile of v1, /device:TPU:0, one launch (start us, length us, event | category | flops | bytes accessed | tf_op | source)
XLA Modules:
  0.0 19.9 jit_solution(16972801887314559951)
XLA Ops:
  0.0 18.5 %shard_map.46 = f32[16,512]{1,0:T(8,128)} custom-call(bf16[128,512]{1,0:T(8,128)(2,1)} %fb_hbm.1, f32[1,128]{1,0:T(1,128)} %bitcast.1, s32[7,128]{1,0:T(8,128)} %ld_hbm.1, s32[3,16]{1,0:T(4,128)} %cd_hbm.1), custom_call_target="tpu_custom_call" | custom-call | tf_op jit(solution)/shard_map/pallas_call | solution.py:252
  18.5 1.4 %copy.6 = f32[16,512]{1,0:T(8,128)} copy(f32[16,512]{1,0:T(8,128)} %shard_map.46) | data formatting | bytes 65536

commit v2 on v1

v2 whole, which is shorter than its diff:
```python
import functools
import math

import jax
import jax.numpy as jnp
from jax import lax
from jax.experimental import pallas as pl
from jax.experimental.pallas import tpu as pltpu
from jax.sharding import PartitionSpec as P

MESH = pl.DeviceIdType.MESH
LANES = 128
SUB = 8
HALF = 15
WINDOW = 31.0


def tiles_of(columns):
    return -(-columns // LANES)


def delayed(tiles, delay, lane, count):
    tiles = tiles[max(0, len(tiles) - count - 1) :]
    source = (lane - delay) & (LANES - 1)
    keep = lane >= delay
    turned = [jnp.take_along_axis(t, source, axis=1, mode="promise_in_bounds") for t in tiles]
    if len(turned) == count:
        turned = [jnp.zeros_like(turned[0])] + turned
    return [jnp.where(keep, turned[k + 1], turned[k]) for k in range(count)]


def merged_right(lower, upper, delay, lane, count):
    source = (lane - delay) & (LANES - 1)
    keep = lane >= delay
    turned = [jnp.take_along_axis(t, source, axis=1, mode="promise_in_bounds") for t in upper]
    zero = jnp.zeros_like(turned[0])
    made = []
    for k in range(count):
        here = turned[k] if k < len(turned) else zero
        left = turned[k - 1] if k else zero
        moved = jnp.where(keep, here, left)
        made.append(lower[k] + moved if k < len(lower) else moved)
    return made


def paired(mine, theirs, on_top, delay, lane, count):
    lower = [jnp.where(on_top, t, m) for t, m in zip(theirs, mine)]
    upper = [jnp.where(on_top, m, t) for t, m in zip(theirs, mine)]
    moved = delayed(upper, delay, lane, count)
    return [a + b for a, b in zip(lower[len(lower) - count :], moved)]


def phases_of(cross_levels):
    phases = []
    for level in range(0, cross_levels, 2):
        one = 1 << level
        phases.append((level, (one, 2 * one, 3 * one) if level + 1 < cross_levels else (one,)))
    return phases


def kernel(
    geometry,
    fb_hbm, bp_hbm, ld_hbm, cd_hbm,
    out_ref,
    fpad, bp_v, ld_v, cd_v, x0, delay_l, delay_c, delay_far, plane, edge_sent, edge_got, sent, got,
    load_sem, edge_send, edge_recv, far_send, far_recv, cross_send, cross_recv,
):
    channels, span, local_levels, cross_levels, trials, shift_max, norm = geometry
    own = span // LANES
    before = tiles_of(cross_levels * shift_max)
    width = before + own
    growth = trials.bit_length() - 1
    row_tiles = trials // SUB
    tm = lax.axis_index("tm")
    sub = lax.axis_index("sub")
    other = 1 - tm
    phases = phases_of(cross_levels)

    barrier = pltpu.get_barrier_semaphore()
    pl.semaphore_signal(barrier, inc=1, device_id={"tm": other}, device_id_type=MESH)
    partners = 1
    for level, masks in phases:
        for mask in masks:
            pl.semaphore_signal(barrier, inc=1, device_id={"sub": sub ^ mask}, device_id_type=MESH)
            partners += 1

    counts = [tiles_of(span + HALF + (m + 1) * shift_max) for m in range(local_levels)]
    start = own + 1
    loads = [
        pltpu.make_async_copy(ld_hbm, ld_v, load_sem.at[0]),
        pltpu.make_async_copy(cd_hbm, cd_v, load_sem.at[1]),
        pltpu.make_async_copy(bp_hbm, bp_v, load_sem.at[2]),
        pltpu.make_async_copy(
            fb_hbm, fpad.at[:, pl.ds(pl.multiple_of(tm * LANES, LANES), span)], load_sem.at[3]
        ),
    ]
    for load in loads:
        load.start()

    @pl.when(tm == 0)
    def _():
        fpad[:, span : start * LANES] = jnp.zeros((channels, LANES), fpad.dtype)
        edge_got[:, : (width - 1) * LANES] = jnp.zeros((trials, (width - 1) * LANES), jnp.float32)

    edge_tiles = counts[-1] - own + before

    @pl.when(tm == 1)
    def _():
        fpad[:, :LANES] = jnp.zeros((channels, LANES), fpad.dtype)
        if edge_tiles < width:
            edge_got[:, edge_tiles * LANES :] = jnp.zeros((trials, (width - edge_tiles) * LANES), jnp.float32)

    for load in loads[:3]:
        load.wait()
    ones = jnp.ones((channels, LANES), jnp.float32).astype(jnp.bfloat16)
    row_at = lax.broadcasted_iota(jnp.int32, (channels, channels), 0)
    col_at = lax.broadcasted_iota(jnp.int32, (channels, channels), 1)
    diagonal = row_at == col_at
    rows = channels
    for level in range(local_levels):
        if level >= growth:
            rows //= 2
        spread = jnp.where(diagonal[:rows], ld_v[level : level + 1, :].astype(jnp.float32), 0.0)
        spread = jnp.dot(spread.astype(jnp.bfloat16), ones, preferred_element_type=jnp.float32)
        delay_l[level, :rows, :] = spread.astype(jnp.int32)
    for level in range(cross_levels):
        spread = jnp.where(diagonal[:trials, :trials], cd_v[level : level + 1, :].astype(jnp.float32), 0.0)
        spread = jnp.dot(spread.astype(jnp.bfloat16), ones[:trials], preferred_element_type=jnp.float32)
        delay_c[level] = spread.astype(jnp.int32)
    gain = jnp.dot(
        jnp.where(diagonal, bp_v[...], 0.0), jnp.ones((channels, LANES), jnp.float32),
        precision=lax.Precision.HIGHEST, preferred_element_type=jnp.float32,
    )
    band_row = lax.broadcasted_iota(jnp.int32, (3 * LANES, LANES), 0)
    band_col = lax.broadcasted_iota(jnp.int32, (3 * LANES, LANES), 1)
    apart = band_row - LANES - band_col
    band = jnp.where((apart >= -HALF) & (apart <= HALF), 1.0, 0.0).astype(jnp.bfloat16)

    loads[3].wait()
    for k in range(start):
        low, high = max(k - 1, 0), min(k + 2, start)
        total = jnp.dot(
            fpad[:, low * LANES : high * LANES], band[(low - k + 1) * LANES : (high - k + 1) * LANES],
            preferred_element_type=jnp.float32,
        )
        centre = fpad[:, k * LANES : (k + 1) * LANES].astype(jnp.float32)
        x0[:, k * LANES : (k + 1) * LANES] = gain * (centre - total / WINDOW)

    lane = lax.broadcasted_iota(jnp.int32, (SUB, LANES), 1)
    sublane = lax.broadcasted_iota(jnp.int32, (SUB, LANES), 0)

    def block(at, carry):
        base = at * trials
        current = []
        for r in range(row_tiles):
            here = pl.ds(pl.multiple_of(base + r * SUB, SUB), SUB)
            current.append([x0[here, k * LANES : (k + 1) * LANES] for k in range(start)])
        for level in range(growth):
            count, step = counts[level], 1 << level
            following = []
            for r in range(row_tiles):
                delay = delay_l[level, pl.ds(pl.multiple_of(base + r * SUB, SUB), SUB), :]
                if step < SUB:
                    is_upper = (sublane & step) != 0
                    lower, upper = [], []
                    for t in current[r]:
                        down = pltpu.roll(t, step, 0)
                        up = down if 2 * step == SUB else pltpu.roll(t, SUB - step, 0)
                        lower.append(jnp.where(is_upper, down, t))
                        upper.append(jnp.where(is_upper, t, up))
                else:
                    apart = step // SUB
                    lower, upper = current[r & ~apart], current[r | apart]
                following.append(merged_right(lower, upper, delay, lane, count))
            current = following
        for r in range(row_tiles):
            here = pl.ds(pl.multiple_of(base + r * SUB, SUB), SUB)
            for k, t in enumerate(current[r]):
                plane[here, k * LANES : (k + 1) * LANES] = t
        return carry

    lax.fori_loop(0, channels // trials, block, 0)

    bands = channels // trials
    count = counts[growth - 1]
    current = [
        [[plane[(b * row_tiles + r) * SUB : (b * row_tiles + r + 1) * SUB, k * LANES : (k + 1) * LANES] for k in range(count)] for r in range(row_tiles)]
        for b in range(bands)
    ]
    for level in range(growth, local_levels):
        count = counts[level]
        bands //= 2
        following = []
        for b in range(bands):
            made = []
            for r in range(row_tiles):
                at = (b * row_tiles + r) * SUB
                delay = delay_l[level, at : at + SUB, :]
                made.append(merged_right(current[2 * b][r], current[2 * b + 1][r], delay, lane, count))
            following.append(made)
        current = following
    frame = current[0]

    for r in range(row_tiles):
        for k, t in enumerate(frame[r]):
            edge_sent[r * SUB : (r + 1) * SUB, k * LANES : (k + 1) * LANES] = t
    pl.semaphore_wait(barrier, partners)

    far_copies = []
    for at, (level, masks) in enumerate(phases):
        if len(masks) > 1:
            copy = pltpu.make_async_remote_copy(
                src_ref=delay_c.at[level], dst_ref=delay_far.at[at],
                send_sem=far_send.at[at], recv_sem=far_recv.at[at],
                device_id={"sub": sub ^ masks[1]}, device_id_type=MESH,
            )
            far_copies.append(copy)

    def edges(r):
        here = pl.ds(r * SUB, SUB)
        onward = pltpu.make_async_remote_copy(
            src_ref=edge_sent.at[here, pl.ds((own - before) * LANES, edge_tiles * LANES)],
            dst_ref=edge_got.at[here, pl.ds(0, edge_tiles * LANES)],
            send_sem=edge_send.at[0, r], recv_sem=edge_recv.at[0, r],
            device_id={"tm": other}, device_id_type=MESH,
        )
        backward = pltpu.make_async_remote_copy(
            src_ref=edge_sent.at[here, pl.ds(0, LANES)],
            dst_ref=edge_got.at[here, pl.ds((width - 1) * LANES, LANES)],
            send_sem=edge_send.at[1, r], recv_sem=edge_recv.at[1, r],
            device_id={"tm": other}, device_id_type=MESH,
        )
        return onward, backward

    edge_copies = [edges(r) for r in range(row_tiles)]

    @pl.when(tm == 0)
    def _():
        for onward, backward in edge_copies:
            onward.start()

    @pl.when(tm == 1)
    def _():
        for onward, backward in edge_copies:
            backward.start()

    for copy in far_copies:
        copy.start()

    copies = []

    def send(at, r, tiles):
        skip = width - len(tiles)
        for k, t in enumerate(tiles, skip):
            sent[at, r * SUB : (r + 1) * SUB, k * LANES : (k + 1) * LANES] = t
        made = []
        for slot, mask in enumerate(phases[at][1]):
            copy = pltpu.make_async_remote_copy(
                src_ref=sent.at[at, pl.ds(r * SUB, SUB), pl.ds(skip * LANES, len(tiles) * LANES)],
                dst_ref=got.at[at, slot, pl.ds(r * SUB, SUB), pl.ds(skip * LANES, len(tiles) * LANES)],
                send_sem=cross_send.at[at, slot, r], recv_sem=cross_recv.at[at, slot, r],
                device_id={"sub": sub ^ mask}, device_id_type=MESH,
            )
            copy.start()
            made.append(copy)
        copies.extend(made)
        return made

    rows_of, flight = [], []
    for r in range(row_tiles):
        onward, backward = edge_copies[r]

        @pl.when(tm == 0)
        def _():
            backward.wait_recv()

        @pl.when(tm == 1)
        def _():
            onward.wait_recv()

        tiles = []
        for t in range(-before, own):
            k = t + before
            piece = edge_got[r * SUB : (r + 1) * SUB, k * LANES : (k + 1) * LANES]
            zero = jnp.zeros_like(piece)
            early = frame[r][t] if t >= 0 else zero
            late = frame[r][t + 1] if t >= -1 else zero
            tiles.append(piece + jnp.where(tm == 1, late, early))
        rows_of.append(tiles)
        if phases:
            flight.append(send(0, r, tiles))

    for at, (level, masks) in enumerate(phases):
        if len(masks) > 1:
            far_copies[[a for a, p in enumerate(phases) if len(p[1]) > 1].index(at)].wait_recv()
        for r in range(row_tiles):
            mine = rows_of[r]
            here = slice(r * SUB, (r + 1) * SUB)
            skip = width - len(mine)

            def landed(slot):
                flight[r][slot].wait_recv()
                return [got[at, slot, here, (k + skip) * LANES : (k + skip + 1) * LANES] for k in range(len(mine))]

            made = paired(mine, landed(0), (sub >> level) & 1 == 1, delay_c[level, here, :], lane, own + tiles_of((cross_levels - level - 1) * shift_max))
            if len(masks) > 1:
                far = paired(landed(1), landed(2), (sub >> level) & 1 == 1, delay_far[at, here, :], lane, len(made))
                made = paired(made, far, (sub >> (level + 1)) & 1 == 1, delay_c[level + 1, here, :], lane, own + tiles_of((cross_levels - level - 2) * shift_max))
            rows_of[r] = made
            if at + 1 < len(phases):
                flight[r] = send(at + 1, r, made)
    for r in range(row_tiles):
        for k, t in enumerate(rows_of[r][-own:]):
            out_ref[r * SUB : (r + 1) * SUB, k * LANES : (k + 1) * LANES] = t * norm
    for copy in copies + far_copies:
        copy.wait_send()

    @pl.when(tm == 0)
    def _():
        for onward, backward in edge_copies:
            onward.wait_send()

    @pl.when(tm == 1)
    def _():
        for onward, backward in edge_copies:
            backward.wait_send()


def shards(filterbank, bandpass, local_delays, cross_delays):
    channels, span = filterbank.shape
    shift_max = span // 16
    local_levels = local_delays.shape[0]
    cross_levels = lax.axis_size("sub").bit_length() - 1
    trials = cross_delays.shape[1]
    norm = 1.0 / math.sqrt(channels * lax.axis_size("sub"))
    own = span // LANES
    width = (own + tiles_of(cross_levels * shift_max)) * LANES
    frame = tiles_of(span + HALF + local_levels * shift_max) * LANES
    phases = max(len(phases_of(cross_levels)), 1)
    row_tiles = trials // SUB
    geometry = (channels, span, local_levels, cross_levels, trials, shift_max, norm)
    return pl.pallas_call(
        functools.partial(kernel, geometry),
        out_shape=jax.ShapeDtypeStruct((trials, span), jnp.float32),
        in_specs=[pl.BlockSpec(memory_space=pl.ANY)] * 4,
        out_specs=pl.BlockSpec(memory_space=pltpu.VMEM),
        scratch_shapes=[
            pltpu.VMEM((channels, (own + 1) * LANES), jnp.bfloat16),
            pltpu.VMEM((1, channels), jnp.float32),
            pltpu.VMEM(local_delays.shape, jnp.int32),
            pltpu.VMEM(cross_delays.shape, jnp.int32),
            pltpu.VMEM((channels, (own + 1) * LANES), jnp.float32),
            pltpu.VMEM((local_levels, channels, LANES), jnp.int32),
            pltpu.VMEM((max(cross_levels, 1), trials, LANES), jnp.int32),
            pltpu.VMEM((phases, trials, LANES), jnp.int32),
            pltpu.VMEM((channels, frame), jnp.float32),
            pltpu.VMEM((trials, frame), jnp.float32),
            pltpu.VMEM((trials, width), jnp.float32),
            pltpu.VMEM((phases, trials, width), jnp.float32),
            pltpu.VMEM((phases, 3, trials, width), jnp.float32),
            pltpu.SemaphoreType.DMA((4,)),
            pltpu.SemaphoreType.DMA((2, row_tiles)),
            pltpu.SemaphoreType.DMA((2, row_tiles)),
            pltpu.SemaphoreType.DMA((phases,)),
            pltpu.SemaphoreType.DMA((phases,)),
            pltpu.SemaphoreType.DMA((phases, 3, row_tiles)),
            pltpu.SemaphoreType.DMA((phases, 3, row_tiles)),
        ],
        compiler_params=pltpu.CompilerParams(collective_id=0, has_side_effects=True),
    )(filterbank, bandpass.reshape(1, channels), local_delays, cross_delays)


def solution(mesh):
    return jax.shard_map(
        shards,
        mesh=mesh,
        in_specs=(P(("beam", "sub"), "tm"), P(("beam", "sub")), P(None, "sub"), P(None, "sub")),
        out_specs=P(("beam", "sub"), "tm"),
        check_vma=False,
    )
```

time: 20.1 us -> 19.1 us (0.950)
  Pallas kernels: 18.5 us -> 17.5 us
    pallas_call x1, Pallas kernels: 18.5 us -> 17.5 us  [shards(): pl.pallas_call(functools.partial(kernel, geometry), out_shape=jax.ShapeDt...]
where the time goes in v2:
time: 19.1 us; the launch traced here: 18.9 us
  Pallas kernels  17.5 us (92%)
  local copies, waits for them, and re-layouts  1.38 us (7%)
    pallas_call x1, Pallas kernels, shards(): pl.pallas_call(functools.partial(kernel, geometry), out_shape=jax.ShapeDt...  17.5 us
    unnamed x1, local copies, waits for them, and re-layouts  1.38 us

profile of v2, /device:TPU:0, one launch (start us, length us, event | category | flops | bytes accessed | tf_op | source)
XLA Modules:
  0.0 18.9 jit_solution(10337155053604592125)
XLA Ops:
  0.0 17.5 %shard_map.46 = f32[16,512]{1,0:T(8,128)} custom-call(bf16[128,512]{1,0:T(8,128)(2,1)} %fb_hbm.1, f32[1,128]{1,0:T(1,128)} %bitcast.1, s32[7,128]{1,0:T(8,128)} %ld_hbm.1, s32[3,16]{1,0:T(4,128)} %cd_hbm.1), custom_call_target="tpu_custom_call" | custom-call | tf_op jit(solution)/shard_map/pallas_call | solution.py:342
  17.5 1.4 %copy.6 = f32[16,512]{1,0:T(8,128)} copy(f32[16,512]{1,0:T(8,128)} %shard_map.46) | data formatting | bytes 65536

commit v3 on v2

--- a/solution.py
+++ b/solution.py
@@ -179,7 +179,7 @@
                 plane[here, k * LANES : (k + 1) * LANES] = t
         return carry
 
-    lax.fori_loop(0, channels // trials, block, 0)
+    lax.fori_loop(0, channels // trials, block, 0, unroll=True)
 
     bands = channels // trials
     count = counts[growth - 1]

time: 19.1 us -> 17.4 us (0.911)
  Pallas kernels: 17.5 us -> 15.8 us
    pallas_call x1, Pallas kernels: 17.5 us -> 15.8 us  [shards(): pl.pallas_call(functools.partial(kernel, geometry), out_shape=jax.ShapeDt...]
where the time goes in v3:
time: 17.4 us; the launch traced here: 17.2 us
  Pallas kernels  15.8 us (91%)
  local copies, waits for them, and re-layouts  1.38 us (8%)
    pallas_call x1, Pallas kernels, shards(): pl.pallas_call(functools.partial(kernel, geometry), out_shape=jax.ShapeDt...  15.8 us
    unnamed x1, local copies, waits for them, and re-layouts  1.38 us

profile of v3, /device:TPU:0, one launch (start us, length us, event | category | flops | bytes accessed | tf_op | source)
XLA Modules:
  0.0 17.2 jit_solution(12638509215978762453)
XLA Ops:
  0.0 15.8 %shard_map.46 = f32[16,512]{1,0:T(8,128)} custom-call(bf16[128,512]{1,0:T(8,128)(2,1)} %fb_hbm.1, f32[1,128]{1,0:T(1,128)} %bitcast.1, s32[7,128]{1,0:T(8,128)} %ld_hbm.1, s32[3,16]{1,0:T(4,128)} %cd_hbm.1), custom_call_target="tpu_custom_call" | custom-call | tf_op jit(solution)/shard_map/pallas_call | solution.py:342
  15.8 1.4 %copy.6 = f32[16,512]{1,0:T(8,128)} copy(f32[16,512]{1,0:T(8,128)} %shard_map.46) | data formatting | bytes 65536

commit v4 on v3

--- a/solution.py
+++ b/solution.py
@@ -341,7 +341,7 @@
     geometry = (channels, span, local_levels, cross_levels, trials, shift_max, norm)
     return pl.pallas_call(
         functools.partial(kernel, geometry),
-        out_shape=jax.ShapeDtypeStruct((trials, span), jnp.float32),
+        out_shape=pltpu.VMEM((trials, span), jnp.float32),
         in_specs=[pl.BlockSpec(memory_space=pl.ANY)] * 4,
         out_specs=pl.BlockSpec(memory_space=pltpu.VMEM),
         scratch_shapes=[

time: 17.4 us -> 16 us (0.920)
  local copies, waits for them, and re-layouts: 1.38 us -> 0.62 us
  Pallas kernels: 15.8 us -> 15.2 us
    unnamed x1, local copies, waits for them, and re-layouts: 1.38 us -> 0.62 us
    pallas_call x1, Pallas kernels: 15.8 us -> 15.2 us  [shards(): pl.pallas_call(functools.partial(kernel, geometry), out_shape=pltpu.VMEM(...]
where the time goes in v4:
time: 16 us; the launch traced here: 15.9 us
  Pallas kernels  15.2 us (95%)
  local copies, waits for them, and re-layouts  0.62 us (4%)
    pallas_call x1, Pallas kernels, shards(): pl.pallas_call(functools.partial(kernel, geometry), out_shape=pltpu.VMEM(...  15.2 us
    unnamed x1, local copies, waits for them, and re-layouts  0.62 us

profile of v4, /device:TPU:0, one launch (start us, length us, event | category | flops | bytes accessed | tf_op | source)
XLA Modules:
  0.0 15.9 jit_solution(5714400889308687758)
XLA Ops:
  0.0 15.2 %shard_map.46 = f32[16,512]{1,0:T(8,128)S(1)} custom-call(bf16[128,512]{1,0:T(8,128)(2,1)} %fb_hbm.1, f32[1,128]{1,0:T(1,128)} %bitcast.1, s32[7,128]{1,0:T(8,128)} %ld_hbm.1, s32[3,16]{1,0:T(4,128)} %cd_hbm.1), custom_call_target="tpu_custom_call" | custom-call | tf_op jit(solution)/shard_map/pallas_call | solution.py:342
  15.2 0.6 %copy.6 = f32[16,512]{1,0:T(8,128)} copy(f32[16,512]{1,0:T(8,128)S(1)} %shard_map.46) | data formatting | bytes 65536

commit v5 on v4

--- a/solution.py
+++ b/solution.py
@@ -83,6 +83,10 @@
         for mask in masks:
             pl.semaphore_signal(barrier, inc=1, device_id={"sub": sub ^ mask}, device_id_type=MESH)
             partners += 1
+    edge_masks = (0,) + (phases[0][1] if phases else ())
+    for mask in edge_masks[1:]:
+        pl.semaphore_signal(barrier, inc=1, device_id={"sub": sub ^ mask, "tm": other}, device_id_type=MESH)
+        partners += 1
 
     counts = [tiles_of(span + HALF + (m + 1) * shift_max) for m in range(local_levels)]
     start = own + 1
@@ -100,7 +104,8 @@
     @pl.when(tm == 0)
     def _():
         fpad[:, span : start * LANES] = jnp.zeros((channels, LANES), fpad.dtype)
-        edge_got[:, : (width - 1) * LANES] = jnp.zeros((trials, (width - 1) * LANES), jnp.float32)
+        for slot in range(len(edge_masks)):
+            edge_got[slot, :, : (width - 1) * LANES] = jnp.zeros((trials, (width - 1) * LANES), jnp.float32)
 
     edge_tiles = counts[-1] - own + before
 
@@ -108,7 +113,8 @@
     def _():
         fpad[:, :LANES] = jnp.zeros((channels, LANES), fpad.dtype)
         if edge_tiles < width:
-            edge_got[:, edge_tiles * LANES :] = jnp.zeros((trials, (width - edge_tiles) * LANES), jnp.float32)
+            for slot in range(len(edge_masks)):
+                edge_got[slot, :, edge_tiles * LANES :] = jnp.zeros((trials, (width - edge_tiles) * LANES), jnp.float32)
 
     for load in loads[:3]:
         load.wait()
@@ -216,33 +222,24 @@
             )
             far_copies.append(copy)
 
-    def edges(r):
+    def edges(r, slot, mask):
         here = pl.ds(r * SUB, SUB)
+        target = {"sub": sub ^ mask, "tm": other} if mask else {"tm": other}
         onward = pltpu.make_async_remote_copy(
             src_ref=edge_sent.at[here, pl.ds((own - before) * LANES, edge_tiles * LANES)],
-            dst_ref=edge_got.at[here, pl.ds(0, edge_tiles * LANES)],
-            send_sem=edge_send.at[0, r], recv_sem=edge_recv.at[0, r],
-            device_id={"tm": other}, device_id_type=MESH,
+            dst_ref=edge_got.at[slot, here, pl.ds(0, edge_tiles * LANES)],
+            send_sem=edge_send.at[0, slot, r], recv_sem=edge_recv.at[0, slot, r],
+            device_id=target, device_id_type=MESH,
         )
         backward = pltpu.make_async_remote_copy(
             src_ref=edge_sent.at[here, pl.ds(0, LANES)],
-            dst_ref=edge_got.at[here, pl.ds((width - 1) * LANES, LANES)],
-            send_sem=edge_send.at[1, r], recv_sem=edge_recv.at[1, r],
-            device_id={"tm": other}, device_id_type=MESH,
+            dst_ref=edge_got.at[slot, here, pl.ds((width - 1) * LANES, LANES)],
+            send_sem=edge_send.at[1, slot, r], recv_sem=edge_recv.at[1, slot, r],
+            device_id=target, device_id_type=MESH,
         )
         return onward, backward
 
-    edge_copies = [edges(r) for r in range(row_tiles)]
-
-    @pl.when(tm == 0)
-    def _():
-        for onward, backward in edge_copies:
-            onward.start()
-
-    @pl.when(tm == 1)
-    def _():
-        for onward, backward in edge_copies:
-            backward.start()
+    edge_copies = [[edges(r, slot, mask) for slot, mask in enumerate(edge_masks)] for r in range(row_tiles)]
 
     for copy in far_copies:
         copy.start()
@@ -266,9 +263,8 @@
         copies.extend(made)
         return made
 
-    rows_of, flight = [], []
-    for r in range(row_tiles):
-        onward, backward = edge_copies[r]
+    def with_edge(r, slot, tiles):
+        onward, backward = edge_copies[r][slot]
 
         @pl.when(tm == 0)
         def _():
@@ -278,18 +274,32 @@
         def _():
             onward.wait_recv()
 
+        return [t + edge_got[slot, r * SUB : (r + 1) * SUB, k * LANES : (k + 1) * LANES] for k, t in enumerate(tiles)]
+
+    rows_of, flight = [], []
+    for r in range(row_tiles):
         tiles = []
         for t in range(-before, own):
-            k = t + before
-            piece = edge_got[r * SUB : (r + 1) * SUB, k * LANES : (k + 1) * LANES]
-            zero = jnp.zeros_like(piece)
+            zero = jnp.zeros_like(frame[r][0])
             early = frame[r][t] if t >= 0 else zero
             late = frame[r][t + 1] if t >= -1 else zero
-            tiles.append(piece + jnp.where(tm == 1, late, early))
+            tiles.append(jnp.where(tm == 1, late, early))
         rows_of.append(tiles)
         if phases:
             flight.append(send(0, r, tiles))
 
+        @pl.when(tm == 0)
+        def _():
+            for onward, backward in edge_copies[r]:
+                onward.start()
+
+        @pl.when(tm == 1)
+        def _():
+            for onward, backward in edge_copies[r]:
+                backward.start()
+
+    for r in range(row_tiles):
+        rows_of[r] = with_edge(r, 0, rows_of[r])
     for at, (level, masks) in enumerate(phases):
         if len(masks) > 1:
             far_copies[[a for a, p in enumerate(phases) if len(p[1]) > 1].index(at)].wait_recv()
@@ -300,7 +310,8 @@
 
             def landed(slot):
                 flight[r][slot].wait_recv()
-                return [got[at, slot, here, (k + skip) * LANES : (k + skip + 1) * LANES] for k in range(len(mine))]
+                tiles = [got[at, slot, here, (k + skip) * LANES : (k + skip + 1) * LANES] for k in range(len(mine))]
+                return tiles if at else with_edge(r, slot + 1, tiles)
 
             made = paired(mine, landed(0), (sub >> level) & 1 == 1, delay_c[level, here, :], lane, own + tiles_of((cross_levels - level - 1) * shift_max))
             if len(masks) > 1:
@@ -317,13 +328,15 @@
 
     @pl.when(tm == 0)
     def _():
-        for onward, backward in edge_copies:
-            onward.wait_send()
+        for row in edge_copies:
+            for onward, backward in row:
+                onward.wait_send()
 
     @pl.when(tm == 1)
     def _():
-        for onward, backward in edge_copies:
-            backward.wait_send()
+        for row in edge_copies:
+            for onward, backward in row:
+                backward.wait_send()
 
 
 def shards(filterbank, bandpass, local_delays, cross_delays):
@@ -355,12 +368,12 @@
             pltpu.VMEM((phases, trials, LANES), jnp.int32),
             pltpu.VMEM((channels, frame), jnp.float32),
             pltpu.VMEM((trials, frame), jnp.float32),
-            pltpu.VMEM((trials, width), jnp.float32),
+            pltpu.VMEM((4, trials, width), jnp.float32),
             pltpu.VMEM((phases, trials, width), jnp.float32),
             pltpu.VMEM((phases, 3, trials, width), jnp.float32),
             pltpu.SemaphoreType.DMA((4,)),
-            pltpu.SemaphoreType.DMA((2, row_tiles)),
-            pltpu.SemaphoreType.DMA((2, row_tiles)),
+            pltpu.SemaphoreType.DMA((2, 4, row_tiles)),
+            pltpu.SemaphoreType.DMA((2, 4, row_tiles)),
             pltpu.SemaphoreType.DMA((phases,)),
             pltpu.SemaphoreType.DMA((phases,)),
             pltpu.SemaphoreType.DMA((phases, 3, row_tiles)),

time: 16 us -> 15.6 us (0.975)
  Pallas kernels: 15.2 us -> 14.8 us
    pallas_call x1, Pallas kernels: 15.2 us -> 14.8 us  [shards(): pl.pallas_call(functools.partial(kernel, geometry), out_shape=pltpu.VMEM(...]
where the time goes in v5:
time: 15.6 us; the launch traced here: 15.4 us
  Pallas kernels  14.8 us (95%)
  local copies, waits for them, and re-layouts  0.62 us (4%)
    pallas_call x1, Pallas kernels, shards(): pl.pallas_call(functools.partial(kernel, geometry), out_shape=pltpu.VMEM(...  14.8 us
    unnamed x1, local copies, waits for them, and re-layouts  0.62 us

profile of v5, /device:TPU:0, one launch (start us, length us, event | category | flops | bytes accessed | tf_op | source)
XLA Modules:
  0.0 15.4 jit_solution(13876256513197226812)
XLA Ops:
  0.0 14.8 %shard_map.46 = f32[16,512]{1,0:T(8,128)S(1)} custom-call(bf16[128,512]{1,0:T(8,128)(2,1)} %fb_hbm.1, f32[1,128]{1,0:T(1,128)} %bitcast.1, s32[7,128]{1,0:T(8,128)} %ld_hbm.1, s32[3,16]{1,0:T(4,128)} %cd_hbm.1), custom_call_target="tpu_custom_call" | custom-call | tf_op jit(solution)/shard_map/pallas_call | solution.py:355
  14.8 0.6 %copy.6 = f32[16,512]{1,0:T(8,128)} copy(f32[16,512]{1,0:T(8,128)S(1)} %shard_map.46) | data formatting | bytes 65536
